TPU v7x, 256 devices: a whole 4x4x8 slice. The times are simulated.
256 devices in a mesh: grp: 8 (over y, core), sub: 32 (over z, x).
Axes of the slice: x: 4, y: 4, z: 8, core: 2. Of those that a mesh axis runs over, the one named last changes fastest.
Arguments:
- schur_block: float32 [8, 32, 1152, 1152], P('grp', 'sub')
- dirichlet_inverse: float32 [8, 32, 1152, 1152], P('grp', 'sub')
- coarse_basis: float32 [8, 32, 24, 1152], P('grp', 'sub'), may hold values from -0.3125 to 0.3125
- coarse_inverse: float32 [8, 768, 768], P('grp', None, 'sub')
- coarse_owner: int32 [8, 768], P('grp', 'sub'), may hold values from 0 to 767, each once within a row
- face_count: int32 [8, 32, 4], P('grp', 'sub'), may hold values from 0 to 384, as said below
- face_rows: int32 [8, 32, 4, 384], P('grp', 'sub'), may hold values from 0 to 1151, as said below
- multiplicity: int32 [8, 32, 1152], P('grp', 'sub'), may hold values from 1 to 5, as said below
- gradient: float32 [8, 32, 192, 1152], P('grp', 'sub'), may hold values from -6 to 6
- warm_start: float32 [8, 32, 192, 1152], P('grp', 'sub'), may hold values from -3 to 3
Outputs:
- adjoint: float32 [8, 32, 192, 1152], P('grp', 'sub')
Inputs may be any that keep to these rules, and one draw needn't show every extreme that they name: `coarse_owner`: each group's row names each coarse unknown once. `face_count`: faces across one grp or sub step have equal counts on both sides; faces 2 and 3 at the ends of sub have count 0; some face has count 384 in every draw. `face_rows`: the live entries of one face are distinct rows; entry k of a face and entry k of the matching face of the neighbour name the same unknown; a row may lie on several faces. `multiplicity`: one plus the number of live face entries that name the row.
All inputs are finite; a program needn't handle non-finite values.
Results may differ from a plain program's by a relative error of at most 0.00023.
Values sent between devices are 32-bit elements; how exact they have to be, the bound alone decides.
A program may use at most 128 MiB of HBM per device.

v0:
```python
import jax
import jax.numpy as jnp
from jax import lax
from jax.sharding import PartitionSpec as P

ITERS = 3


HIGHEST = lax.Precision.HIGHEST


def shifted(array, axis, by):
    peers = lax.axis_size(axis)
    return lax.ppermute(array, axis, [(i, (i + by) % peers) for i in range(peers)])


def from_behind(value, axis, steps):
    count = lax.axis_size(axis)
    first, last = (max(0, -steps), min(count, count - steps))
    return lax.ppermute(value, axis, [(source, source + steps) for source in range(first, last)])


def product(left, right):
    return jnp.dot(left, right, precision=HIGHEST, preferred_element_type=jnp.float32)


def local(
    schur_block,
    dirichlet_inverse,
    coarse_basis,
    coarse_inverse,
    coarse_owner,
    face_count,
    face_rows,
    multiplicity,
    gradient,
    warm_start,
):
    schur_local = schur_block[0, 0]
    dirichlet_local = dirichlet_inverse[0, 0]
    coarse_rows = coarse_basis[0, 0]
    face_index = face_rows[0, 0]
    live_mask = (jnp.arange(face_index.shape[1])[None, :] < face_count[0, 0][:, None]).astype(
        jnp.float32
    )
    weight = (1.0 / multiplicity[0, 0].astype(jnp.float32))[None, :]
    my_owner = coarse_owner[0]
    all_owner = lax.all_gather(coarse_owner, "sub", axis=1, tiled=True)[0]

    def assemble(values):
        outgoing = jax.vmap(lambda one_index, one_mask: values[:, one_index] * one_mask[None, :])(
            face_index, live_mask
        )
        from_next = shifted(outgoing[1], "grp", -1)
        from_prev = shifted(outgoing[0], "grp", 1)
        from_after = from_behind(outgoing[3], "sub", -1)
        from_before = from_behind(outgoing[2], "sub", 1)
        values = values.at[:, face_index[0]].add(from_next)
        values = values.at[:, face_index[1]].add(from_prev)
        values = values.at[:, face_index[2]].add(from_after)
        return values.at[:, face_index[3]].add(from_before)

    adjoint = warm_start[0, 0]
    right_side = gradient[0, 0]
    for iteration in range(ITERS):
        applied = product(adjoint, schur_local)
        residual = right_side - assemble(applied)
        weighted = residual * weight
        local_part = product(weighted, dirichlet_local)
        coarse_piece = lax.dot_general(
            weighted,
            coarse_rows,
            (((1,), (1,)), ((), ())),
            precision=HIGHEST,
            preferred_element_type=jnp.float32,
        )
        pieces = lax.all_gather(coarse_piece, "sub", axis=1, tiled=True)
        coarse_sum = jnp.zeros_like(pieces).at[:, all_owner].set(pieces)
        owned = product(coarse_sum, coarse_inverse[0])
        gathered = lax.all_gather(owned, "sub", axis=1, tiled=True)
        picked = gathered[:, my_owner]
        correction = product(picked, coarse_rows)
        adjoint = adjoint + assemble((local_part + correction) * weight)
    return adjoint[None, None]


def solution(mesh):
    in_specs = (
        P("grp", "sub", None, None),
        P("grp", "sub", None, None),
        P("grp", "sub", None, None),
        P("grp", None, "sub"),
        P("grp", "sub"),
        P("grp", "sub", None),
        P("grp", "sub", None, None),
        P("grp", "sub", None),
        P("grp", "sub", None, None),
        P("grp", "sub", None, None),
    )
    out_specs = P("grp", "sub", None, None)
    return jax.shard_map(local, mesh=mesh, in_specs=in_specs, out_specs=out_specs, check_vma=False)
```

profile of v0, /device:TPU:1, one launch (start us, length us, event | category | flops | bytes accessed | tf_op | source)
XLA Modules:
  0.0 631.9 jit_solution(7648857142585618406)
XLA Ops:
  1.5 11.3 %fusion.10 = f32[192,1152]{0,1:T(8,128)S(1)} fusion(f32[1,1,1152,1152]{3,2,1,0:T(8,128)} %param.10, f32[1,1,192,1152]{3,2,1,0:T(8,128)} %param.19), kind=kOutput, calls=%fused_computation.46 | convolution fusion | flops 3057647616 | bytes 7077888 | tf_op jit(solution)/shard_map/dot_general | solution.py:24
  12.8 4.7 gather_fusion
  19.3 4.0 collective-permute-start.3
  28.1 22.5 %all-reduce = s32[768]{0:T(1024)S(1)} all-reduce(s32[768]{0:T(1024)S(1)} %bitcast_dynamic-update-slice_fusion), channel_id=1, replica_groups=mesh['grp'=8,'sub'=32] {'sub'}, use_global_device_ids=true, to_apply=%add | all-reduce | flops 768 | bytes 6144
  50.7 3.6 scatter_custom_fusion
  54.3 3.7 scatter_custom_fusion.1
  58.1 3.6 scatter_custom_fusion.2
  66.9 36.0 %all_gather.22 = f32[192,768]{0,1:T(8,128)S(1)} all-gather(f32[192,24]{0,1:T(8,128)S(1)} %fusion.97), channel_id=1, replica_groups=mesh['grp'=8,'sub'=32] {'sub'}, dimensions={1}, use_global_device_ids=true | all-gather | bytes 608256 | tf_op jit(solution)/shard_map/all_gather | solution.py:77
  102.9 6.3 scatter_custom_fusion.4
  110.9 41.2 %all_gather.23 = f32[192,768]{0,1:T(8,128)} all-gather(f32[192,24]{0,1:T(8,128)S(1)} %fusion.113), channel_id=1, replica_groups=mesh['grp'=8,'sub'=32] {'sub'}, dimensions={1}, use_global_device_ids=true | all-gather | bytes 608256 | tf_op jit(solution)/shard_map/all_gather | solution.py:80
  154.7 8.0 %bitcast_add_fusion = (f32[192,1152]{1,0:T(8,128)}, f32[192,1152]{1,0:T(8,128)}) fusion(f32[1,1,192,1152]{3,2,1,0:T(8,128)S(1)} %copy-done.6, f32[1152]{0:T(1024)S(1)} %divide_reduce_fusion, f32[192,1152]{1,0:T(8,128)S(1)} %fusion.106, f32[1,1,1152,1152]{3,2,1,0:T(8,128)} %param.11, f32[192,1152]{1,0:T(8,128)S(1)} %copy.31, ...), kind=kOutput, calls=%fused_computation.66 | convolution fusion | flops 3058753536 | bytes 10621440 | tf_op jit(solution)/shard_map/dot_general | solution.py:24
  164.2 4.7 gather_fusion.2
  171.8 28.8 %collective-permute-start.4 = (f32[192,384]{0,1:T(8,128)}, f32[192,384]{0,1:T(8,128)}, u32[]{:S(2)}, u32[]{:S(2)}) collective-permute-start(f32[192,384]{0,1:T(8,128)} %get-tuple-element.28), channel_id=1, source_target_pairs={{0,224},{32,0},{64,32},{96,64},{128,96},{160,128},{192,160},{224,1... | collective-permute-start | bytes 884744 | tf_op jit(solution)/shard_map/ppermute | solution.py:14
  203.0 4.7 collective-permute-start.7
  208.1 3.6 scatter_custom_fusion.5
  218.9 4.0 scatter_custom_fusion.8
  222.9 11.1 %fusion.8 = f32[192,1152]{0,1:T(8,128)S(1)} fusion(f32[192,1152]{0,1:T(8,128)S(1)} %scatter_custom_fusion.8, f32[1,1,1152,1152]{3,2,1,0:T(8,128)} %param.10), kind=kOutput, calls=%fused_computation.44 | convolution fusion | flops 3057647616 | bytes 7077888 | tf_op jit(solution)/shard_map/dot_general | solution.py:24
  234.0 4.7 gather_fusion.3
  244.4 4.8 collective-permute-start.11
  252.8 3.7 scatter_custom_fusion.10
  256.5 3.6 scatter_custom_fusion.11
  260.1 3.6 scatter_custom_fusion.12
  267.1 39.6 %all_gather.24 = f32[192,768]{0,1:T(8,128)S(1)} all-gather(f32[192,24]{0,1:T(8,128)S(1)} %fusion.94), channel_id=1, replica_groups=mesh['grp'=8,'sub'=32] {'sub'}, dimensions={1}, use_global_device_ids=true | all-gather | bytes 608256 | tf_op jit(solution)/shard_map/all_gather | solution.py:77
  306.6 6.3 scatter_custom_fusion.13
  314.6 42.3 %all_gather.25 = f32[192,768]{0,1:T(8,128)} all-gather(f32[192,24]{0,1:T(8,128)S(1)} %fusion.111), channel_id=1, replica_groups=mesh['grp'=8,'sub'=32] {'sub'}, dimensions={1}, use_global_device_ids=true | all-gather | bytes 608256 | tf_op jit(solution)/shard_map/all_gather | solution.py:80
  359.6 7.7 %fusion.24 = f32[192,1152]{1,0:T(8,128)} fusion(f32[192,1152]{1,0:T(8,128)S(1)} %fusion.103, f32[1,1,1152,1152]{3,2,1,0:T(8,128)} %param.11, f32[1152]{0:T(1024)S(1)} %divide_reduce_fusion, f32[192,1152]{1,0:T(8,128)S(1)} %copy-done.3, f32[1,1,192,1152]{3,2,1,0:T(8,128)S(1)} %copy-done.1), kind=kOutput, calls=%fused_computation.52 | convolution fusion | flops 3058532352 | bytes 8851968 | tf_op jit(solution)/shard_map/dot_general | solution.py:24
  368.8 4.7 gather_fusion.5
  376.3 24.3 %collective-permute-start.12 = (f32[192,384]{0,1:T(8,128)}, f32[192,384]{0,1:T(8,128)}, u32[]{:S(2)}, u32[]{:S(2)}) collective-permute-start(f32[192,384]{0,1:T(8,128)} %get-tuple-element.20), channel_id=1, source_target_pairs={{0,224},{32,0},{64,32},{96,64},{128,96},{160,128},{192,160},{224,1... | collective-permute-start | bytes 884744 | tf_op jit(solution)/shard_map/ppermute | solution.py:14
  402.7 4.7 collective-permute-start.15
  412.4 3.6 scatter_custom_fusion.14
  416.0 3.6 scatter_custom_fusion.15
  419.6 3.6 scatter_custom_fusion.16
  423.2 4.0 scatter_custom_fusion.17
  427.2 11.1 %fusion.6 = f32[192,1152]{0,1:T(8,128)S(1)} fusion(f32[192,1152]{0,1:T(8,128)S(1)} %scatter_custom_fusion.17, f32[1,1,1152,1152]{3,2,1,0:T(8,128)} %param.10), kind=kOutput, calls=%fused_computation.42 | convolution fusion | flops 3057647616 | bytes 7077888 | tf_op jit(solution)/shard_map/dot_general | solution.py:24
  438.3 4.7 gather_fusion.6
  448.7 4.8 collective-permute-start.19
  457.1 3.7 scatter_custom_fusion.19
  460.8 3.6 scatter_custom_fusion.20
  464.4 3.6 scatter_custom_fusion.21
  471.3 40.6 %all_gather.26 = f32[192,768]{0,1:T(8,128)S(1)} all-gather(f32[192,24]{0,1:T(8,128)S(1)} %fusion.91), channel_id=1, replica_groups=mesh['grp'=8,'sub'=32] {'sub'}, dimensions={1}, use_global_device_ids=true | all-gather | bytes 608256 | tf_op jit(solution)/shard_map/all_gather | solution.py:77
  511.9 6.3 scatter_custom_fusion.22
  519.9 42.2 %all_gather.27 = f32[192,768]{0,1:T(8,128)} all-gather(f32[192,24]{0,1:T(8,128)S(1)} %fusion.109), channel_id=1, replica_groups=mesh['grp'=8,'sub'=32] {'sub'}, dimensions={1}, use_global_device_ids=true | all-gather | bytes 608256 | tf_op jit(solution)/shard_map/all_gather | solution.py:80
  564.8 7.7 %fusion.21 = f32[192,1152]{1,0:T(8,128)} fusion(f32[192,1152]{1,0:T(8,128)S(1)} %fusion.100, f32[1,1,1152,1152]{3,2,1,0:T(8,128)} %param.11, f32[1152]{0:T(1024)S(1)} %divide_reduce_fusion, f32[192,1152]{1,0:T(8,128)S(1)} %copy-done.2, f32[1,1,192,1152]{3,2,1,0:T(8,128)S(1)} %copy-done.1), kind=kOutput, calls=%fused_computation.51 | convolution fusion | flops 3058532352 | bytes 8851968 | tf_op jit(solution)/shard_map/dot_general | solution.py:24
  574.0 4.7 gather_fusion.8
  581.3 24.9 %collective-permute-start.20 = (f32[192,384]{0,1:T(8,128)}, f32[192,384]{0,1:T(8,128)}, u32[]{:S(2)}, u32[]{:S(2)}) collective-permute-start(f32[192,384]{0,1:T(8,128)} %get-tuple-element.12), channel_id=1, source_target_pairs={{0,224},{32,0},{64,32},{96,64},{128,96},{160,128},{192,160},{224,1... | collective-permute-start | bytes 884744 | tf_op jit(solution)/shard_map/ppermute | solution.py:14
  608.0 4.7 collective-permute-start.23
  615.7 3.6 scatter_custom_fusion.23
  622.8 3.8 scatter_custom_fusion.25
  (122 shorter events, 93.8 us)
Async XLA Ops:
  0.0 65.2 %copy-start = (f32[1,1,24,1152]{3,2,1,0:T(8,128)S(1)}, f32[1,1,24,1152]{3,2,1,0:T(8,128)}, u32[]{:S(2)}) copy-start(f32[1,1,24,1152]{3,2,1,0:T(8,128)} %param.12) | copy-start | bytes 331780
  19.1 7.6 %copy-start.11 = (s32[1,24]{1,0:T(1,128)S(1)}, s32[1,24]{1,0:T(1,128)}, u32[]{:S(2)}) copy-start(s32[1,24]{1,0:T(1,128)} %param.14) | copy-start | bytes 292
  19.2 7.6 %copy-start.12 = (u32[256]{0:T(256)S(1)}, u32[256]{0:T(256)}, u32[]{:S(2)}) copy-start(u32[256]{0:T(256)} %constant.27) | copy-start | bytes 3076
  19.2 31.5 %copy-start.9 = (s32[1,1,4,384]{3,2,1,0:T(4,128)S(1)}, s32[1,1,4,384]{3,2,1,0:T(4,128)}, u32[]{:S(2)}) copy-start(s32[1,1,4,384]{3,2,1,0:T(4,128)} %param.16) | copy-start | bytes 18436
  19.2 31.5 %copy-start.10 = (s32[1,1,1152]{2,1,0:T(1,128)S(1)}, s32[1,1,1152]{2,1,0:T(1,128)}, u32[]{:S(2)}) copy-start(s32[1,1,1152]{2,1,0:T(1,128)} %param.17) | copy-start | bytes 13828
  19.3 42.3 %collective-permute-start.3 = (f32[192,384]{0,1:T(8,128)S(1)}, f32[192,384]{0,1:T(8,128)S(1)}, u32[]{:S(2)}, u32[]{:S(2)}) collective-permute-start(f32[192,384]{0,1:T(8,128)S(1)} %get-tuple-element.29), channel_id=1, source_target_pairs={{0,1},{1,2},{2,3},{3,4},{4,5},{5,6},{6,7},{7,8},{8,9},{9,10},{10,1... | collective-permute-start | bytes 884744 | tf_op jit(solution)/shard_map/ppermute | solution.py:20
  23.3 34.8 %collective-permute-start.2 = (f32[192,384]{0,1:T(8,128)S(1)}, f32[192,384]{0,1:T(8,128)}, u32[]{:S(2)}, u32[]{:S(2)}) collective-permute-start(f32[192,384]{0,1:T(8,128)S(1)} %get-tuple-element.30), channel_id=1, source_target_pairs={{1,0},{2,1},{3,2},{4,3},{5,4},{6,5},{7,6},{8,7},{9,8},{10,9},{11,1... | collective-permute-start | bytes 884744 | tf_op jit(solution)/shard_map/ppermute | solution.py:20
  24.6 29.7 %collective-permute-start.1 = (f32[192,384]{0,1:T(8,128)S(1)}, f32[192,384]{0,1:T(8,128)}, u32[]{:S(2)}, u32[]{:S(2)}) collective-permute-start(f32[192,384]{0,1:T(8,128)S(1)} %get-tuple-element.31), channel_id=1, source_target_pairs={{0,32},{32,64},{64,96},{96,128},{128,160},{160,192},{192,224},{224... | collective-permute-start | bytes 884744 | tf_op jit(solution)/shard_map/ppermute | solution.py:14
  26.7 24.0 %collective-permute-start = (f32[192,384]{0,1:T(8,128)S(1)}, f32[192,384]{0,1:T(8,128)}, u32[]{:S(2)}, u32[]{:S(2)}) collective-permute-start(f32[192,384]{0,1:T(8,128)S(1)} %get-tuple-element.32), channel_id=1, source_target_pairs={{0,224},{32,0},{64,32},{96,64},{128,96},{160,128},{192,160},{224,1... | collective-permute-start | bytes 884744 | tf_op jit(solution)/shard_map/ppermute | solution.py:14
  64.8 1.2 copy-start.1
  66.9 42.4 %copy-start.8 = (f32[1,768,24]{1,2,0:T(8,128)S(1)}, f32[1,768,24]{1,2,0:T(8,128)}, u32[]{:S(2)}) copy-start(f32[1,768,24]{1,2,0:T(8,128)} %param.13) | copy-start | bytes 221188
  110.8 43.8 %copy-start.6 = (f32[1,1,192,1152]{3,2,1,0:T(8,128)S(1)}, f32[1,1,192,1152]{3,2,1,0:T(8,128)}, u32[]{:S(2)}) copy-start(f32[1,1,192,1152]{3,2,1,0:T(8,128)} %param.19) | copy-start | bytes 2654212
  170.6 37.2 %copy-start.7 = (f32[192,1152]{1,0:T(8,128)S(1)}, f32[192,1152]{1,0:T(8,128)}, u32[]{:S(2)}) copy-start(f32[192,1152]{1,0:T(8,128)} %get-tuple-element.33) | copy-start | bytes 2654212
  171.8 36.4 %collective-permute-start.4 = (f32[192,384]{0,1:T(8,128)}, f32[192,384]{0,1:T(8,128)}, u32[]{:S(2)}, u32[]{:S(2)}) collective-permute-start(f32[192,384]{0,1:T(8,128)} %get-tuple-element.28), channel_id=1, source_target_pairs={{0,224},{32,0},{64,32},{96,64},{128,96},{160,128},{192,160},{224,1... | collective-permute-start | bytes 884744 | tf_op jit(solution)/shard_map/ppermute | solution.py:14
  200.6 11.1 %collective-permute-start.5 = (f32[192,384]{0,1:T(8,128)}, f32[192,384]{0,1:T(8,128)}, u32[]{:S(2)}, u32[]{:S(2)}) collective-permute-start(f32[192,384]{0,1:T(8,128)} %get-tuple-element.27), channel_id=1, source_target_pairs={{0,32},{32,64},{64,96},{96,128},{128,160},{160,192},{192,224},{224... | collective-permute-start | bytes 884744 | tf_op jit(solution)/shard_map/ppermute | solution.py:14
  201.7 13.6 %collective-permute-start.6 = (f32[192,384]{0,1:T(8,128)}, f32[192,384]{0,1:T(8,128)}, u32[]{:S(2)}, u32[]{:S(2)}) collective-permute-start(f32[192,384]{0,1:T(8,128)} %get-tuple-element.26), channel_id=1, source_target_pairs={{1,0},{2,1},{3,2},{4,3},{5,4},{6,5},{7,6},{8,7},{9,8},{10,9},{11,1... | collective-permute-start | bytes 884744 | tf_op jit(solution)/shard_map/ppermute | solution.py:20
  203.0 15.9 %collective-permute-start.7 = (f32[192,384]{0,1:T(8,128)}, f32[192,384]{0,1:T(8,128)}, u32[]{:S(2)}, u32[]{:S(2)}) collective-permute-start(f32[192,384]{0,1:T(8,128)} %get-tuple-element.25), channel_id=1, source_target_pairs={{0,1},{1,2},{2,3},{3,4},{4,5},{5,6},{6,7},{7,8},{8,9},{9,10},{10,1... | collective-permute-start | bytes 884744 | tf_op jit(solution)/shard_map/ppermute | solution.py:20
  241.4 7.8 %collective-permute-start.8 = (f32[192,384]{0,1:T(8,128)S(1)}, f32[192,384]{0,1:T(8,128)}, u32[]{:S(2)}, u32[]{:S(2)}) collective-permute-start(f32[192,384]{0,1:T(8,128)S(1)} %get-tuple-element.24), channel_id=1, source_target_pairs={{0,224},{32,0},{64,32},{96,64},{128,96},{160,128},{192,160},{224,1... | collective-permute-start | bytes 884744 | tf_op jit(solution)/shard_map/ppermute | solution.py:14
  241.4 11.4 %collective-permute-start.9 = (f32[192,384]{0,1:T(8,128)}, f32[192,384]{0,1:T(8,128)}, u32[]{:S(2)}, u32[]{:S(2)}) collective-permute-start(f32[192,384]{0,1:T(8,128)} %get-tuple-element.23), channel_id=1, source_target_pairs={{0,32},{32,64},{64,96},{96,128},{128,160},{160,192},{192,224},{224... | collective-permute-start | bytes 884744 | tf_op jit(solution)/shard_map/ppermute | solution.py:14
  243.1 13.4 %collective-permute-start.10 = (f32[192,384]{0,1:T(8,128)}, f32[192,384]{0,1:T(8,128)}, u32[]{:S(2)}, u32[]{:S(2)}) collective-permute-start(f32[192,384]{0,1:T(8,128)} %get-tuple-element.22), channel_id=1, source_target_pairs={{1,0},{2,1},{3,2},{4,3},{5,4},{6,5},{7,6},{8,7},{9,8},{10,9},{11,1... | collective-permute-start | bytes 884744 | tf_op jit(solution)/shard_map/ppermute | solution.py:20
  244.4 15.7 %collective-permute-start.11 = (f32[192,384]{0,1:T(8,128)}, f32[192,384]{0,1:T(8,128)}, u32[]{:S(2)}, u32[]{:S(2)}) collective-permute-start(f32[192,384]{0,1:T(8,128)} %get-tuple-element.21), channel_id=1, source_target_pairs={{0,1},{1,2},{2,3},{3,4},{4,5},{5,6},{6,7},{7,8},{8,9},{9,10},{10,1... | collective-permute-start | bytes 884744 | tf_op jit(solution)/shard_map/ppermute | solution.py:20
  314.6 45.0 %copy-start.3 = (f32[192,1152]{1,0:T(8,128)S(1)}, f32[192,1152]{1,0:T(8,128)}, u32[]{:S(2)}) copy-start(f32[192,1152]{1,0:T(8,128)} %copy.36) | copy-start | bytes 2654212
  376.3 32.4 %copy-start.5 = (f32[192,1152]{1,0:T(8,128)S(1)}, f32[192,1152]{1,0:T(8,128)}, u32[]{:S(2)}) copy-start(f32[192,1152]{1,0:T(8,128)} %fusion.24) | copy-start | bytes 2654212
  376.3 36.1 %collective-permute-start.12 = (f32[192,384]{0,1:T(8,128)}, f32[192,384]{0,1:T(8,128)}, u32[]{:S(2)}, u32[]{:S(2)}) collective-permute-start(f32[192,384]{0,1:T(8,128)} %get-tuple-element.20), channel_id=1, source_target_pairs={{0,224},{32,0},{64,32},{96,64},{128,96},{160,128},{192,160},{224,1... | collective-permute-start | bytes 884744 | tf_op jit(solution)/shard_map/ppermute | solution.py:14
  400.6 15.4 %collective-permute-start.13 = (f32[192,384]{0,1:T(8,128)}, f32[192,384]{0,1:T(8,128)}, u32[]{:S(2)}, u32[]{:S(2)}) collective-permute-start(f32[192,384]{0,1:T(8,128)} %get-tuple-element.19), channel_id=1, source_target_pairs={{0,32},{32,64},{64,96},{96,128},{128,160},{160,192},{192,224},{224... | collective-permute-start | bytes 884744 | tf_op jit(solution)/shard_map/ppermute | solution.py:14
  401.4 18.2 %collective-permute-start.14 = (f32[192,384]{0,1:T(8,128)}, f32[192,384]{0,1:T(8,128)}, u32[]{:S(2)}, u32[]{:S(2)}) collective-permute-start(f32[192,384]{0,1:T(8,128)} %get-tuple-element.18), channel_id=1, source_target_pairs={{1,0},{2,1},{3,2},{4,3},{5,4},{6,5},{7,6},{8,7},{9,8},{10,9},{11,1... | collective-permute-start | bytes 884744 | tf_op jit(solution)/shard_map/ppermute | solution.py:20
  402.7 20.5 %collective-permute-start.15 = (f32[192,384]{0,1:T(8,128)}, f32[192,384]{0,1:T(8,128)}, u32[]{:S(2)}, u32[]{:S(2)}) collective-permute-start(f32[192,384]{0,1:T(8,128)} %get-tuple-element.17), channel_id=1, source_target_pairs={{0,1},{1,2},{2,3},{3,4},{4,5},{5,6},{6,7},{7,8},{8,9},{9,10},{10,1... | collective-permute-start | bytes 884744 | tf_op jit(solution)/shard_map/ppermute | solution.py:20
  445.7 7.8 %collective-permute-start.16 = (f32[192,384]{0,1:T(8,128)S(1)}, f32[192,384]{0,1:T(8,128)}, u32[]{:S(2)}, u32[]{:S(2)}) collective-permute-start(f32[192,384]{0,1:T(8,128)S(1)} %get-tuple-element.16), channel_id=1, source_target_pairs={{0,224},{32,0},{64,32},{96,64},{128,96},{160,128},{192,160},{224,1... | collective-permute-start | bytes 884744 | tf_op jit(solution)/shard_map/ppermute | solution.py:14
  446.0 11.0 %collective-permute-start.17 = (f32[192,384]{0,1:T(8,128)}, f32[192,384]{0,1:T(8,128)}, u32[]{:S(2)}, u32[]{:S(2)}) collective-permute-start(f32[192,384]{0,1:T(8,128)} %get-tuple-element.15), channel_id=1, source_target_pairs={{0,32},{32,64},{64,96},{96,128},{128,160},{160,192},{192,224},{224... | collective-permute-start | bytes 884744 | tf_op jit(solution)/shard_map/ppermute | solution.py:14
  447.4 13.4 %collective-permute-start.18 = (f32[192,384]{0,1:T(8,128)}, f32[192,384]{0,1:T(8,128)}, u32[]{:S(2)}, u32[]{:S(2)}) collective-permute-start(f32[192,384]{0,1:T(8,128)} %get-tuple-element.14), channel_id=1, source_target_pairs={{1,0},{2,1},{3,2},{4,3},{5,4},{6,5},{7,6},{8,7},{9,8},{10,9},{11,1... | collective-permute-start | bytes 884744 | tf_op jit(solution)/shard_map/ppermute | solution.py:20
  448.7 15.7 %collective-permute-start.19 = (f32[192,384]{0,1:T(8,128)}, f32[192,384]{0,1:T(8,128)}, u32[]{:S(2)}, u32[]{:S(2)}) collective-permute-start(f32[192,384]{0,1:T(8,128)} %get-tuple-element.13), channel_id=1, source_target_pairs={{0,1},{1,2},{2,3},{3,4},{4,5},{5,6},{6,7},{7,8},{8,9},{9,10},{10,1... | collective-permute-start | bytes 884744 | tf_op jit(solution)/shard_map/ppermute | solution.py:20
  519.9 44.9 %copy-start.2 = (f32[192,1152]{1,0:T(8,128)S(1)}, f32[192,1152]{1,0:T(8,128)}, u32[]{:S(2)}) copy-start(f32[192,1152]{1,0:T(8,128)} %copy.42) | copy-start | bytes 2654212
  581.3 31.7 %copy-start.4 = (f32[192,1152]{1,0:T(8,128)S(1)}, f32[192,1152]{1,0:T(8,128)}, u32[]{:S(2)}) copy-start(f32[192,1152]{1,0:T(8,128)} %fusion.21) | copy-start | bytes 2654212
  581.3 34.3 %collective-permute-start.20 = (f32[192,384]{0,1:T(8,128)}, f32[192,384]{0,1:T(8,128)}, u32[]{:S(2)}, u32[]{:S(2)}) collective-permute-start(f32[192,384]{0,1:T(8,128)} %get-tuple-element.12), channel_id=1, source_target_pairs={{0,224},{32,0},{64,32},{96,64},{128,96},{160,128},{192,160},{224,1... | collective-permute-start | bytes 884744 | tf_op jit(solution)/shard_map/ppermute | solution.py:14
  606.2 13.0 %collective-permute-start.21 = (f32[192,384]{0,1:T(8,128)}, f32[192,384]{0,1:T(8,128)}, u32[]{:S(2)}, u32[]{:S(2)}) collective-permute-start(f32[192,384]{0,1:T(8,128)} %get-tuple-element.11), channel_id=1, source_target_pairs={{0,32},{32,64},{64,96},{96,128},{128,160},{160,192},{192,224},{224... | collective-permute-start | bytes 884744 | tf_op jit(solution)/shard_map/ppermute | solution.py:14
  606.7 16.1 %collective-permute-start.22 = (f32[192,384]{0,1:T(8,128)}, f32[192,384]{0,1:T(8,128)}, u32[]{:S(2)}, u32[]{:S(2)}) collective-permute-start(f32[192,384]{0,1:T(8,128)} %get-tuple-element.10), channel_id=1, source_target_pairs={{1,0},{2,1},{3,2},{4,3},{5,4},{6,5},{7,6},{8,7},{9,8},{10,9},{11,1... | collective-permute-start | bytes 884744 | tf_op jit(solution)/shard_map/ppermute | solution.py:20
  608.0 18.6 %collective-permute-start.23 = (f32[192,384]{0,1:T(8,128)S(1)}, f32[192,384]{0,1:T(8,128)}, u32[]{:S(2)}, u32[]{:S(2)}) collective-permute-start(f32[192,384]{0,1:T(8,128)S(1)} %get-tuple-element.9), channel_id=1, source_target_pairs={{0,1},{1,2},{2,3},{3,4},{4,5},{5,6},{6,7},{7,8},{8,9},{9,10},{10,1... | collective-permute-start | bytes 884744 | tf_op jit(solution)/shard_map/ppermute | solution.py:20
where the time goes:
time: 643 us; the launch traced here: 632 us
  blocking collectives  264 us (41%)
  starting transfers between devices  121 us (19%)
  other arithmetic  101 us (16%)
  local copies, waits for them, and re-layouts  73 us (11%)
  matrix products  69.6 us (11%)
    all_gather x3, blocking collectives, local(): gathered = lax.all_gather(owned, 'sub', axis=1, tiled=True)  126 us
    all_gather x3, blocking collectives, local(): pieces = lax.all_gather(coarse_piece, 'sub', axis=1, tiled=True)  116 us
    ppermute x12, starting transfers between devices, shifted(): lax.ppermute(array, axis, [(i, (i + by) % peers) for i in range(peers)])  86.1 us
    dot_general x12, matrix products, product(): jnp.dot(left, right, precision=HIGHEST, preferred_element_type=jnp.float32)  64.5 us
    ppermute x12, starting transfers between devices, from_behind(): lax.ppermute(value, axis, [(source, source + steps) for source in range(f...  35.4 us
    gather x6, local copies, waits for them, and re-layouts, assemble(): values[:, one_index] * one_mask[None, :]  27.9 us
    unnamed x1, blocking collectives  22.5 us
    scatter-add x6, other arithmetic, assemble(): values = values.at[:, face_index[1]].add(from_prev)  21.9 us
  transfers between devices with their start and end apart: 24, of which 0 were waited for; matrix products, arithmetic and copies ran while one was open for 12% of the time, Pallas kernels for 0%

commit v1 on v0

v1 whole, which is shorter than its diff:
```python
import functools

import jax
import jax.numpy as jnp
from jax import lax
from jax.experimental import pallas as pl
from jax.experimental.pallas import tpu as pltpu
from jax.sharding import PartitionSpec as P

ITERS = 3
NI = 1152
FMAX = 384
NCL = 24
RHS = 192
GROUPS = 8
SUBS = 32
CG = 768
BF = jnp.bfloat16
F32 = jnp.float32
HIGHEST = lax.Precision.HIGHEST
MESH = pl.DeviceIdType.MESH
NN = (((1,), (0,)), ((), ()))
NT = (((1,), (1,)), ((), ()))
TN = (((0,), (0,)), ((), ()))


def parts(value):
    high = value.astype(BF)
    return high, (value - high.astype(F32)).astype(BF)


def dot(left, right, dims=NN):
    return lax.dot_general(left, right, dims, preferred_element_type=F32)


def three(left, right, dims):
    left_high, left_low = parts(left)
    right_high, right_low = parts(right)
    return (
        dot(left_high, right_high, dims)
        + dot(left_low, right_high, dims)
        + dot(left_high, right_low, dims)
    )


def kernel(
    schur_high, schur_low, dirichlet_high, dirichlet_low, basis, mixing, pick, place, weight,
    gradient, warm, out,
    adjoint, values, stacked, send, recv, pieces, face_sent, face_got, piece_sent, piece_got,
):
    grp = lax.axis_index("grp")
    sub = lax.axis_index("sub")
    around = (lax.rem(grp + 1, GROUPS), lax.rem(grp + GROUPS - 1, GROUPS))
    along = (lax.rem(sub + 1, SUBS), lax.rem(sub + SUBS - 1, SUBS))
    targets = (
        (around[0], sub),
        (around[1], sub),
        (grp, along[0]),
        (grp, along[1]),
    )

    barrier = pltpu.get_barrier_semaphore()
    for target in targets[:2]:
        pl.semaphore_signal(barrier, inc=1, device_id=target, device_id_type=MESH)

    def greet(step, carry):
        pl.semaphore_signal(
            barrier, inc=1, device_id=(grp, lax.rem(sub + step, SUBS)), device_id_type=MESH
        )
        return carry

    lax.fori_loop(1, SUBS, greet, 0)
    pl.semaphore_wait(barrier, SUBS + 1)

    def stack(value):
        rows = value.shape[0]
        high, low = parts(value)
        return jnp.concatenate([high, low], axis=0)

    def product(source, high, low):
        stacked[...] = stack(source)
        for start, size in ((0, 512), (512, 640)):
            both = dot(stacked[...], high[:, start : start + size])
            values[:, start : start + size] = (
                both[:RHS] + both[RHS:] + dot(stacked[:RHS], low[:, start : start + size])
            )

    def face_copy(phase, face):
        return pltpu.make_async_remote_copy(
            src_ref=send.at[face],
            dst_ref=recv.at[phase, face ^ 1],
            send_sem=face_sent.at[phase, face],
            recv_sem=face_got.at[phase, face ^ 1],
            device_id=targets[face],
            device_id_type=MESH,
        )

    def assemble(phase):
        stacked[...] = stack(values[...])
        for pair in (1, 0):
            both = dot(stacked[...], pick[pair])
            chosen = both[:RHS] + both[RHS:]
            for side in (0, 1):
                send[2 * pair + side] = chosen[:, side * FMAX : (side + 1) * FMAX]
                face_copy(phase, 2 * pair + side).start()
        for pair in (0, 1):
            for side in (0, 1):
                pltpu.make_async_remote_copy(
                    src_ref=send.at[2 * pair + side],
                    dst_ref=recv.at[phase, 2 * pair + side],
                    send_sem=face_sent.at[phase, 2 * pair + side],
                    recv_sem=face_got.at[phase, 2 * pair + side],
                    device_id=targets[2 * pair + side],
                    device_id_type=MESH,
                ).wait_recv()
            arrived = stack(
                jnp.concatenate([recv[phase, 2 * pair], recv[phase, 2 * pair + 1]], axis=1)
            )
            both = dot(arrived, place[pair])
            values[...] += both[:RHS] + both[RHS:]
        for face in range(4):
            face_copy(phase, face).wait_send()

    adjoint[...] = warm[...]

    def iterate(iteration, carry):
        product(adjoint[...], schur_high, schur_low)
        assemble(2 * iteration)
        weighted = (gradient[...] - values[...]) * weight[...]
        pieces[iteration, sub] = three(basis[...], weighted, NT)

        def piece_copy(step, landing):
            return pltpu.make_async_remote_copy(
                src_ref=pieces.at[iteration, sub],
                dst_ref=pieces.at[iteration, landing],
                send_sem=piece_sent.at[iteration, step],
                recv_sem=piece_got.at[iteration, step],
                device_id=(grp, lax.rem(sub + step, SUBS)),
                device_id_type=MESH,
            )

        def launch(step, carry):
            piece_copy(step, sub).start()
            return carry

        lax.fori_loop(1, SUBS, launch, 0)
        product(weighted, dirichlet_high, dirichlet_low)

        def land(step, carry):
            piece_copy(step, lax.rem(sub + SUBS - step, SUBS)).wait_recv()
            return carry

        lax.fori_loop(1, SUBS, land, 0)
        gathered = pieces[iteration].reshape(CG, RHS)
        picked = three(mixing[...], gathered, NN)
        values[...] = (values[...] + three(picked, basis[...], TN)) * weight[...]
        assemble(2 * iteration + 1)
        adjoint[...] += values[...]

        def leave(step, carry):
            piece_copy(step, sub).wait_send()
            return carry

        lax.fori_loop(1, SUBS, leave, 0)
        return carry

    lax.fori_loop(0, ITERS, iterate, 0)
    out[...] = adjoint[...]


def split(matrix):
    high = lax.reduce_precision(matrix, 8, 7)
    return high.astype(BF), (matrix - high).astype(BF)


def local(
    schur_block,
    dirichlet_inverse,
    coarse_basis,
    coarse_inverse,
    coarse_owner,
    face_count,
    face_rows,
    multiplicity,
    gradient,
    warm_start,
):
    my_owner = coarse_owner[0]
    all_owner = lax.all_gather(coarse_owner, "sub", axis=1, tiled=True)[0]
    inverse_columns = lax.all_gather(coarse_inverse[0].T, "sub", axis=0, tiled=True)
    order = (jnp.arange(CG)[:, None] == all_owner[None, :]).astype(F32)
    mixing = jnp.dot(inverse_columns[my_owner], order, precision=HIGHEST, preferred_element_type=F32)

    face_index = face_rows[0, 0]
    live = jnp.arange(FMAX)[None, :] < face_count[0, 0][:, None]
    masked = jnp.where(live, face_index, NI).reshape(2, 2 * FMAX)
    rows = jnp.arange(NI)
    pick = (rows[None, :, None] == masked[:, None, :]).astype(BF)
    place = (masked[:, :, None] == rows[None, None, :]).astype(BF)
    weight = (1.0 / multiplicity[0, 0].astype(F32))[None, :]
    schur_high, schur_low = split(schur_block[0, 0])
    dirichlet_high, dirichlet_low = split(dirichlet_inverse[0, 0])

    vmem = pl.BlockSpec(memory_space=pltpu.VMEM)
    out = pl.pallas_call(
        kernel,
        out_shape=jax.ShapeDtypeStruct((RHS, NI), F32),
        in_specs=[vmem] * 11,
        out_specs=vmem,
        scratch_shapes=[
            pltpu.VMEM((RHS, NI), F32),
            pltpu.VMEM((RHS, NI), F32),
            pltpu.VMEM((2 * RHS, NI), BF),
            pltpu.VMEM((4, RHS, FMAX), F32),
            pltpu.VMEM((2 * ITERS, 4, RHS, FMAX), F32),
            pltpu.VMEM((ITERS, SUBS, NCL, RHS), F32),
            pltpu.SemaphoreType.DMA((2 * ITERS, 4)),
            pltpu.SemaphoreType.DMA((2 * ITERS, 4)),
            pltpu.SemaphoreType.DMA((ITERS, SUBS)),
            pltpu.SemaphoreType.DMA((ITERS, SUBS)),
        ],
        compiler_params=pltpu.CompilerParams(
            collective_id=0, has_side_effects=True, vmem_limit_bytes=60 * 1024 * 1024
        ),
    )(
        schur_high, schur_low, dirichlet_high, dirichlet_low, coarse_basis[0, 0], mixing, pick, place,
        weight, gradient[0, 0], warm_start[0, 0],
    )
    return out[None, None]


def solution(mesh):
    in_specs = (
        P("grp", "sub", None, None),
        P("grp", "sub", None, None),
        P("grp", "sub", None, None),
        P("grp", None, "sub"),
        P("grp", "sub"),
        P("grp", "sub", None),
        P("grp", "sub", None, None),
        P("grp", "sub", None),
        P("grp", "sub", None, None),
        P("grp", "sub", None, None),
    )
    out_specs = P("grp", "sub", None, None)
    return jax.shard_map(local, mesh=mesh, in_specs=in_specs, out_specs=out_specs, check_vma=False)
```

time: 643 us -> 259 us (0.40); the launches traced: 632 us -> 259 us
  blocking collectives: 264 us -> 19.8 us
  Pallas kernels: 0 us -> 158 us
  starting transfers between devices: 121 us -> 0.01 us
  other arithmetic: 101 us -> 16.6 us
  matrix products: 69.6 us -> 1.48 us
  local copies, waits for them, and re-layouts: 73 us -> 7.88 us
  waiting for transfers between devices: 0.06 us -> 41.4 us
  between operations: 1.94 us -> 14.1 us
    all_gather x6 -> x0, blocking collectives: 242 us -> none  [the longest x3 126 us: local(): gathered = lax.all_gather(owned, 'sub', axis=1, tiled=True)]
    pallas_call x0 -> x1, Pallas kernels: none -> 158 us  [local(): pl.pallas_call(kernel, out_shape=jax.ShapeDtypeStruct((RHS, NI), F32), in...]
    ppermute x24 -> x0, starting transfers between devices: 121 us -> none  [the longest x12 86.1 us: shifted(): lax.ppermute(array, axis, [(i, (i + by) % peers) for i in range(peers)])]
    scatter-add x24 -> x0, other arithmetic: 86.6 us -> none  [the longest x6 21.9 us: assemble(): values = values.at[:, face_index[1]].add(from_prev)]
    dot_general x15 -> x1, matrix products: 69.6 us -> 1.48 us  [local(): jnp.dot(inverse_columns[my_owner], order, precision=HIGHEST, preferred_el...]
    all_gather x0 -> x1, waiting for transfers between devices: none -> 40.7 us  [local(): lax.all_gather(coarse_inverse[0].T, 'sub', axis=0, tiled=True)]
    gather x9 -> x1, local copies, waits for them, and re-layouts: 33.1 us -> 2.29 us  [local(): inverse_columns[my_owner]]
    scatter x3 -> x0, local copies, waits for them, and re-layouts: 18.9 us -> none  [local(): coarse_sum = jnp.zeros_like(pieces).at[:, all_owner].set(pieces)]
  transfers between devices with their start and end apart: 24 -> 1, of which waited for: 0 -> 1; matrix products, arithmetic and copies ran while one was open for 12% -> 8% of each run, Pallas kernels for 0% -> 0%
where the time goes in v1:
time: 259 us
  Pallas kernels  158 us (61%)
  waiting for transfers between devices  41.4 us (16%)
  blocking collectives  19.8 us (8%)
  other arithmetic  16.6 us (6%)
  between operations  14.1 us (5%)
  local copies, waits for them, and re-layouts  7.88 us (3%)
    pallas_call x1, Pallas kernels, local(): pl.pallas_call(kernel, out_shape=jax.ShapeDtypeStruct((RHS, NI), F32), in...  158 us
    all_gather x1, waiting for transfers between devices, local(): lax.all_gather(coarse_inverse[0].T, 'sub', axis=0, tiled=True)  40.7 us
    unnamed x1, blocking collectives  19.8 us
    convert_element_type x1, other arithmetic, split(): return (high.astype(BF), (matrix - high).astype(BF))  7.71 us
  transfers between devices with their start and end apart: 1, of which 1 were waited for; matrix products, arithmetic and copies ran while one was open for 8% of the time, Pallas kernels for 0%

profile of v1, /device:TPU:1, one launch (start us, length us, event | category | flops | bytes accessed | tf_op | source)
XLA Modules:
  0.0 259.0 jit_solution(5380375808721462500)
XLA Ops:
  6.5 0.0 all-gather.2.cloned.1.call-start
  6.5 0.7 all-gather.2.cloned.1.call-update
  7.3 0.5 broadcast.66
  7.8 1.3 reduce.3
  9.1 0.1 lt.51
  9.2 0.7 fusion.6
  9.9 1.3 dynamic-slice
  11.8 0.8 bitcast_dynamic-update-slice_fusion
  12.6 19.8 %all-reduce = s32[768]{0:T(1024)S(1)} all-reduce(s32[768]{0:T(1024)S(1)} %bitcast_dynamic-update-slice_fusion), channel_id=1, replica_groups=mesh['grp'=8,'sub'=32] {'sub'}, use_global_device_ids=true, to_apply=%add | all-reduce | flops 768 | bytes 6144
  32.4 0.1 broadcast_bitcast_fusion
  32.5 0.7 squeeze.30
  33.2 1.3 divide_bitcast_fusion.weight
  34.5 0.0 copy-start
  34.5 2.5 fusion.1.place
  37.0 3.2 %fusion.pick = bf16[2,1152,768]{2,1,0:T(8,128)(2,1)} fusion(s32[2,768]{1,0:T(2,128)S(1)} %get-tuple-element.10), kind=kLoop, calls=%fused_computation.7 | loop fusion | flops 3538944 | bytes 3545088 | tf_op jit(solution)/shard_map/convert_element_type | solution.py:198
  40.2 0.0 copy-done
  40.2 7.7 %fusion.2 = (bf16[1152,1152]{1,0:T(8,128)(2,1)}, bf16[1152,1152]{1,0:T(8,128)(2,1)}, bf16[1152,1152]{1,0:T(8,128)(2,1)}, bf16[1152,1152]{1,0:T(8,128)(2,1)}) fusion(f32[1,1,1152,1152]{3,2,1,0:T(8,128)S(1)} %copy-done, f32[1,1,1152,1152]{3,2,1,0:T(8,128)} %param.11), kind=kLoop, calls=%fused_computation.9 | loop fusion | flops 10616832 | bytes 21233664 | tf_op jit(solution)/shard_map/convert_element_type | solution.py:173
  47.9 40.7 %all-gather.2.cloned.1.call-done = f32[768,768]{1,0:T(8,128)} async-done(((f32[24,768]{1,0:T(8,128)}), f32[768,768]{1,0:T(8,128)}) %all-gather.2.cloned.1.call-update) | async-done | bytes 2359312 | tf_op jit(solution)/shard_map/all_gather | solution.py:190
  88.6 2.3 gather_fusion
  90.9 1.5 fusion.4.mixing
  92.3 157.6 %shard_map.100 = f32[192,1152]{1,0:T(8,128)} custom-call(bf16[1152,1152]{1,0:T(8,128)(2,1)} %get-tuple-element.8.schur_high, bf16[1152,1152]{1,0:T(8,128)(2,1)} %get-tuple-element.7.schur_low, bf16[1152,1152]{1,0:T(8,128)(2,1)} %get-tuple-element.11.dirichlet_high, bf16[1152,1152]{1,0:T(8,128)(2,1)} %get-tuple-element.12.dirichlet_low, f32[24,1152]{1,0:T(8,128)} %bitcast.31, ...), custom_call_target="tpu_custom_call" | custom-call | tf_op jit(solution)/shard_map/pallas_call | solution.py:205
  250.0 2.1 copy.14
  (8 shorter events, 0.1 us)
Async XLA Ops:
  6.5 82.0 %all-gather.2.cloned.1.call-start = ((), (), s32[]{:S(2)}) async-start(), calls=%async_computation | async-start | bytes 2433024 | tf_op jit(solution)/shard_map/all_gather | solution.py:190
  34.5 5.6 %copy-start = (f32[1,1,1152,1152]{3,2,1,0:T(8,128)S(1)}, f32[1,1,1152,1152]{3,2,1,0:T(8,128)}, u32[]{:S(2)}) copy-start(f32[1,1,1152,1152]{3,2,1,0:T(8,128)} %param.10) | copy-start | bytes 15925252
Sparse Core Ops, SparseCore 0:
  9.9 78.5 all-gather.1

commit v2 on v1

--- a/solution.py
+++ b/solution.py
@@ -44,12 +44,15 @@
 
 
 def kernel(
-    schur_high, schur_low, dirichlet_high, dirichlet_low, basis, mixing, pick, place, weight,
-    gradient, warm, out,
-    adjoint, values, stacked, send, recv, pieces, face_sent, face_got, piece_sent, piece_got,
+    schur, dirichlet, basis, inverse_block, my_owner, row_of, column_of, weight,
+    gradient, warm, adjoint,
+    schur_high, schur_low, dirichlet_high, dirichlet_low, pick, place, mixing, inverse,
+    values, stacked, send, recv, pieces, face_sent, face_got, piece_sent, piece_got,
+    inverse_sent, inverse_got, own_sem,
 ):
     grp = lax.axis_index("grp")
     sub = lax.axis_index("sub")
+    across = lax.rem(sub, 4)
     around = (lax.rem(grp + 1, GROUPS), lax.rem(grp + GROUPS - 1, GROUPS))
     along = (lax.rem(sub + 1, SUBS), lax.rem(sub + SUBS - 1, SUBS))
     targets = (
@@ -59,18 +62,113 @@
         (grp, along[1]),
     )
 
+    def down(step):
+        return (grp, lax.rem(sub + 4 * step, SUBS))
+
+    def aside(step):
+        return (grp, sub - across + lax.rem(across + step, 4))
+
     barrier = pltpu.get_barrier_semaphore()
-    for target in targets[:2]:
+    greeted = targets + tuple(down(step) for step in range(1, 8)) + tuple(aside(step) for step in range(1, 4))
+    for target in greeted:
         pl.semaphore_signal(barrier, inc=1, device_id=target, device_id_type=MESH)
-
-    def greet(step, carry):
-        pl.semaphore_signal(
-            barrier, inc=1, device_id=(grp, lax.rem(sub + step, SUBS)), device_id_type=MESH
+    pltpu.make_async_copy(inverse_block, inverse.at[sub], own_sem).start()
+    pltpu.make_async_copy(inverse_block, inverse.at[sub], own_sem).wait()
+    pl.semaphore_wait(barrier, len(greeted))
+
+    def owner_down(step):
+        return lax.rem(sub + SUBS - 4 * step, SUBS)
+
+    def owner_aside(step, over):
+        start = sub - across + lax.rem(across + 4 - over, 4)
+        return lax.rem(start + SUBS - 4 * step, SUBS)
+
+    def block_copy(buffer, sent, got, source, landing, step, over, target):
+        return pltpu.make_async_remote_copy(
+            src_ref=buffer.at[source],
+            dst_ref=buffer.at[landing],
+            send_sem=sent.at[4 * step + over],
+            recv_sem=got.at[4 * step + over],
+            device_id=target,
+            device_id_type=MESH,
         )
-        return carry
-
-    lax.fori_loop(1, SUBS, greet, 0)
-    pl.semaphore_wait(barrier, SUBS + 1)
+
+    def gather_start(buffer, sent, got):
+        def body(step, carry):
+            block_copy(buffer, sent, got, sub, sub, step, 0, down(step)).start()
+            return carry
+
+        lax.fori_loop(1, 8, body, 0)
+
+    def relay(buffer, sent, got, step):
+        owner = owner_down(step)
+        for over in (1, 3, 2):
+            block_copy(buffer, sent, got, owner, owner, step, over, aside(over)).start()
+
+    def gather_relay(buffer, sent, got):
+        relay(buffer, sent, got, 0)
+
+        def body(position, carry):
+            step = lax.rem(position, 2) * (8 - (position + 1) // 2) + (1 - lax.rem(position, 2)) * (position // 2)
+            owner = owner_down(step)
+            block_copy(buffer, sent, got, owner, owner, step, 0, down(step)).wait_recv()
+            relay(buffer, sent, got, step)
+            return carry
+
+        lax.fori_loop(1, 8, body, 0)
+
+    def gather_finish(buffer, sent, got):
+        def body(step, carry):
+            for over in (1, 2, 3):
+                owner = owner_aside(step, over)
+                block_copy(buffer, sent, got, owner, owner, step, over, aside(over)).wait_recv()
+            return carry
+
+        lax.fori_loop(0, 8, body, 0)
+
+    def gather_leave(buffer, sent, got):
+        def one(step, carry):
+            block_copy(buffer, sent, got, sub, sub, step, 0, down(step)).wait_send()
+            return carry
+
+        lax.fori_loop(1, 8, one, 0)
+
+        def body(step, carry):
+            owner = owner_down(step)
+            for over in (1, 2, 3):
+                block_copy(buffer, sent, got, owner, owner, step, over, aside(over)).wait_send()
+            return carry
+
+        lax.fori_loop(0, 8, body, 0)
+
+    gather_start(inverse, inverse_sent, inverse_got)
+
+    def split(matrix, high_ref, low_ref):
+        def body(step, carry):
+            rows = pl.ds(pl.multiple_of(step * 128, 128), 128)
+            high_ref[rows, :], low_ref[rows, :] = parts(matrix[rows, :])
+            return carry
+
+        lax.fori_loop(0, NI // 128, body, 0)
+
+    split(schur, schur_high, schur_low)
+    for pair in (0, 1):
+
+        def pick_rows(step, carry):
+            first = pl.multiple_of(step * 128, 128)
+            names = first + lax.broadcasted_iota(jnp.int32, (128, 2 * FMAX), 0)
+            pick[pair, pl.ds(first, 128), :] = jnp.where(names == row_of[pair], 1.0, 0.0).astype(BF)
+            return carry
+
+        lax.fori_loop(0, NI // 128, pick_rows, 0)
+
+        def place_rows(step, carry):
+            rows = pl.ds(pl.multiple_of(step * 128, 128), 128)
+            names = lax.broadcasted_iota(jnp.int32, (128, NI), 1)
+            place[pair, rows, :] = jnp.where(names == column_of[pair, rows, :], 1.0, 0.0).astype(BF)
+            return carry
+
+        lax.fori_loop(0, 2 * FMAX // 128, place_rows, 0)
 
     def stack(value):
         rows = value.shape[0]
@@ -95,7 +193,7 @@
             device_id_type=MESH,
         )
 
-    def assemble(phase):
+    def assemble(phase, between):
         stacked[...] = stack(values[...])
         for pair in (1, 0):
             both = dot(stacked[...], pick[pair])
@@ -103,6 +201,7 @@
             for side in (0, 1):
                 send[2 * pair + side] = chosen[:, side * FMAX : (side + 1) * FMAX]
                 face_copy(phase, 2 * pair + side).start()
+        between()
         for pair in (0, 1):
             for side in (0, 1):
                 pltpu.make_async_remote_copy(
@@ -123,54 +222,50 @@
 
     adjoint[...] = warm[...]
 
+    def mix():
+        gather_finish(inverse, inverse_sent, inverse_got)
+        everyone = inverse[...].reshape(CG, CG + 128)
+        names = lax.broadcasted_iota(jnp.int32, (CG, CG), 1).astype(F32)
+        order = jnp.where(names == everyone[:, CG : CG + 1], 1.0, 0.0).astype(BF)
+        mine = jnp.where(
+            lax.broadcasted_iota(jnp.int32, (NCL, CG), 1) == my_owner[...], 1.0, 0.0
+        ).astype(BF)
+        high, low = parts(everyone[:, :CG])
+        columns = dot(mine, high) + dot(mine, low)
+        high, low = parts(columns)
+        mixing[...] = dot(high, order, NT) + dot(low, order, NT)
+
     def iterate(iteration, carry):
+        block = (pieces.at[iteration], piece_sent.at[iteration], piece_got.at[iteration])
         product(adjoint[...], schur_high, schur_low)
-        assemble(2 * iteration)
+
+        def first_wait():
+            @pl.when(iteration == 0)
+            def _():
+                split(dirichlet, dirichlet_high, dirichlet_low)
+                gather_relay(inverse, inverse_sent, inverse_got)
+
+        assemble(2 * iteration, first_wait)
         weighted = (gradient[...] - values[...]) * weight[...]
         pieces[iteration, sub] = three(basis[...], weighted, NT)
-
-        def piece_copy(step, landing):
-            return pltpu.make_async_remote_copy(
-                src_ref=pieces.at[iteration, sub],
-                dst_ref=pieces.at[iteration, landing],
-                send_sem=piece_sent.at[iteration, step],
-                recv_sem=piece_got.at[iteration, step],
-                device_id=(grp, lax.rem(sub + step, SUBS)),
-                device_id_type=MESH,
-            )
-
-        def launch(step, carry):
-            piece_copy(step, sub).start()
-            return carry
-
-        lax.fori_loop(1, SUBS, launch, 0)
+        gather_start(*block)
         product(weighted, dirichlet_high, dirichlet_low)
-
-        def land(step, carry):
-            piece_copy(step, lax.rem(sub + SUBS - step, SUBS)).wait_recv()
-            return carry
-
-        lax.fori_loop(1, SUBS, land, 0)
+        gather_relay(*block)
+
+        @pl.when(iteration == 0)
+        def _():
+            mix()
+
+        gather_finish(*block)
         gathered = pieces[iteration].reshape(CG, RHS)
         picked = three(mixing[...], gathered, NN)
         values[...] = (values[...] + three(picked, basis[...], TN)) * weight[...]
-        assemble(2 * iteration + 1)
+        assemble(2 * iteration + 1, lambda: gather_leave(*block))
         adjoint[...] += values[...]
-
-        def leave(step, carry):
-            piece_copy(step, sub).wait_send()
-            return carry
-
-        lax.fori_loop(1, SUBS, leave, 0)
         return carry
 
     lax.fori_loop(0, ITERS, iterate, 0)
-    out[...] = adjoint[...]
-
-
-def split(matrix):
-    high = lax.reduce_precision(matrix, 8, 7)
-    return high.astype(BF), (matrix - high).astype(BF)
+    gather_leave(inverse, inverse_sent, inverse_got)
 
 
 def local(
@@ -185,30 +280,29 @@
     gradient,
     warm_start,
 ):
-    my_owner = coarse_owner[0]
-    all_owner = lax.all_gather(coarse_owner, "sub", axis=1, tiled=True)[0]
-    inverse_columns = lax.all_gather(coarse_inverse[0].T, "sub", axis=0, tiled=True)
-    order = (jnp.arange(CG)[:, None] == all_owner[None, :]).astype(F32)
-    mixing = jnp.dot(inverse_columns[my_owner], order, precision=HIGHEST, preferred_element_type=F32)
-
-    face_index = face_rows[0, 0]
+    my_owner = coarse_owner[0][:, None]
+    inverse_block = jnp.concatenate(
+        [coarse_inverse[0].T, jnp.broadcast_to(my_owner.astype(F32), (NCL, 128))], axis=1
+    )
     live = jnp.arange(FMAX)[None, :] < face_count[0, 0][:, None]
-    masked = jnp.where(live, face_index, NI).reshape(2, 2 * FMAX)
-    rows = jnp.arange(NI)
-    pick = (rows[None, :, None] == masked[:, None, :]).astype(BF)
-    place = (masked[:, :, None] == rows[None, None, :]).astype(BF)
+    masked = jnp.where(live, face_rows[0, 0], NI).reshape(2, 2 * FMAX)
     weight = (1.0 / multiplicity[0, 0].astype(F32))[None, :]
-    schur_high, schur_low = split(schur_block[0, 0])
-    dirichlet_high, dirichlet_low = split(dirichlet_inverse[0, 0])
 
     vmem = pl.BlockSpec(memory_space=pltpu.VMEM)
     out = pl.pallas_call(
         kernel,
         out_shape=jax.ShapeDtypeStruct((RHS, NI), F32),
-        in_specs=[vmem] * 11,
+        in_specs=[vmem] * 10,
         out_specs=vmem,
         scratch_shapes=[
-            pltpu.VMEM((RHS, NI), F32),
+            pltpu.VMEM((NI, NI), BF),
+            pltpu.VMEM((NI, NI), BF),
+            pltpu.VMEM((NI, NI), BF),
+            pltpu.VMEM((NI, NI), BF),
+            pltpu.VMEM((2, NI, 2 * FMAX), BF),
+            pltpu.VMEM((2, 2 * FMAX, NI), BF),
+            pltpu.VMEM((NCL, CG), F32),
+            pltpu.VMEM((SUBS, NCL, CG + 128), F32),
             pltpu.VMEM((RHS, NI), F32),
             pltpu.VMEM((2 * RHS, NI), BF),
             pltpu.VMEM((4, RHS, FMAX), F32),
@@ -218,13 +312,16 @@
             pltpu.SemaphoreType.DMA((2 * ITERS, 4)),
             pltpu.SemaphoreType.DMA((ITERS, SUBS)),
             pltpu.SemaphoreType.DMA((ITERS, SUBS)),
+            pltpu.SemaphoreType.DMA((SUBS,)),
+            pltpu.SemaphoreType.DMA((SUBS,)),
+            pltpu.SemaphoreType.DMA,
         ],
         compiler_params=pltpu.CompilerParams(
-            collective_id=0, has_side_effects=True, vmem_limit_bytes=60 * 1024 * 1024
+            collective_id=0, has_side_effects=True, vmem_limit_bytes=63 * 1024 * 1024
         ),
     )(
-        schur_high, schur_low, dirichlet_high, dirichlet_low, coarse_basis[0, 0], mixing, pick, place,
-        weight, gradient[0, 0], warm_start[0, 0],
+        schur_block[0, 0], dirichlet_inverse[0, 0], coarse_basis[0, 0], inverse_block, my_owner,
+        masked[:, None, :], masked[:, :, None], weight, gradient[0, 0], warm_start[0, 0],
     )
     return out[None, None]
 

time: 259 us -> 184 us (0.71)
  waiting for transfers between devices: 41.4 us -> 0 us
  blocking collectives: 19.8 us -> 0 us
  between operations: 14.1 us -> 0.03 us
  Pallas kernels: 158 us -> 170 us
  other arithmetic: 16.6 us -> 6.44 us
    all_gather x1 -> x0, waiting for transfers between devices: 40.7 us -> none  [local(): lax.all_gather(coarse_inverse[0].T, 'sub', axis=0, tiled=True)]
    unnamed x1 -> x0, blocking collectives: 19.8 us -> none
    convert_element_type x3 -> x1, other arithmetic: 13.3 us -> 0.66 us  [local(): my_owner.astype(F32)]
    pallas_call x1, Pallas kernels: 158 us -> 170 us  [local(): pl.pallas_call(kernel, out_shape=jax.ShapeDtypeStruct((RHS, NI), F32), in...]
  transfers between devices with their start and end apart: 1 -> 0, of which waited for: 1 -> 0; matrix products, arithmetic and copies ran while one was open for 8% -> 0% of each run, Pallas kernels for 0% -> 0%
where the time goes in v2:
time: 184 us
  Pallas kernels  170 us (92%)
  local copies, waits for them, and re-layouts  6.92 us (4%)
  other arithmetic  6.44 us (4%)
    pallas_call x1, Pallas kernels, local(): pl.pallas_call(kernel, out_shape=jax.ShapeDtypeStruct((RHS, NI), F32), in...  170 us

profile of v2, /device:TPU:1, one launch (start us, length us, event | category | flops | bytes accessed | tf_op | source)
XLA Modules:
  0.0 183.7 jit_solution(2243947273412177671)
XLA Ops:
  0.0 0.5 broadcast.61
  0.5 1.3 reduce.3
  1.8 0.1 lt.48
  1.9 0.7 convert_bitcast_fusion
  2.6 1.3 divide_bitcast_fusion.weight
  3.9 0.1 lt.49
  4.0 0.7 squeeze.28
  4.7 0.6 compare_select_fusion.1.row_of
  5.3 0.1 broadcast_in_dim.16
  5.4 1.3 copy.14.my_owner
  6.7 1.5 pad_maximum_fusion.inverse_block
  8.2 0.6 lt.57
  8.9 1.3 squeeze.32
  10.2 1.0 compare_select_fusion.column_of
  11.2 170.3 %shard_map.100 = f32[192,1152]{1,0:T(8,128)} custom-call(f32[1152,1152]{1,0:T(8,128)} %bitcast.16, f32[1152,1152]{1,0:T(8,128)} %bitcast.17, f32[24,1152]{1,0:T(8,128)} %bitcast.21, f32[24,896]{1,0:T(8,128)} %pad_maximum_fusion.inverse_block, s32[24,1]{1,0:T(8,128)} %copy.14.my_owner, s32[2,1,768]{2,1,0:T(1,128)} %compare_select_fusion.1.row_of, ...), custom_call_target="tpu_custom_call" | custom-call | tf_op jit(solution)/shard_map/pallas_call | solution.py:292
  181.5 2.1 %copy.16 = f32[1,1,192,1152]{3,2,1,0:T(8,128)} copy(f32[1,1,192,1152]{3,2,1,0:T(8,128)} %bitcast.18) | data formatting | bytes 1769472
  (5 shorter events, 0.1 us)

commit v3 on v2

--- a/solution.py
+++ b/solution.py
@@ -100,16 +100,25 @@
 
         lax.fori_loop(1, 8, body, 0)
 
+    def nearest(position):
+        odd = lax.rem(position, 2)
+        return odd * (8 - (position + 1) // 2) + (1 - odd) * (position // 2)
+
+    def far_copy(buffer, sent, got, step):
+        side = 1 + 2 * lax.rem(step, 2)
+        owner = owner_aside(step, side)
+        return block_copy(buffer, sent, got, owner, owner, step, 2, aside(side))
+
     def relay(buffer, sent, got, step):
         owner = owner_down(step)
-        for over in (1, 3, 2):
+        for over in (1, 3):
             block_copy(buffer, sent, got, owner, owner, step, over, aside(over)).start()
 
     def gather_relay(buffer, sent, got):
         relay(buffer, sent, got, 0)
 
         def body(position, carry):
-            step = lax.rem(position, 2) * (8 - (position + 1) // 2) + (1 - lax.rem(position, 2)) * (position // 2)
+            step = nearest(position)
             owner = owner_down(step)
             block_copy(buffer, sent, got, owner, owner, step, 0, down(step)).wait_recv()
             relay(buffer, sent, got, step)
@@ -117,9 +126,20 @@
 
         lax.fori_loop(1, 8, body, 0)
 
+    def gather_forward(buffer, sent, got):
+        def body(position, carry):
+            step = nearest(position)
+            side = 1 + 2 * lax.rem(step, 2)
+            owner = owner_aside(step, side)
+            block_copy(buffer, sent, got, owner, owner, step, side, aside(side)).wait_recv()
+            far_copy(buffer, sent, got, step).start()
+            return carry
+
+        lax.fori_loop(0, 8, body, 0)
+
     def gather_finish(buffer, sent, got):
         def body(step, carry):
-            for over in (1, 2, 3):
+            for over in (3 - 2 * lax.rem(step, 2), 2):
                 owner = owner_aside(step, over)
                 block_copy(buffer, sent, got, owner, owner, step, over, aside(over)).wait_recv()
             return carry
@@ -135,8 +155,9 @@
 
         def body(step, carry):
             owner = owner_down(step)
-            for over in (1, 2, 3):
+            for over in (1, 3):
                 block_copy(buffer, sent, got, owner, owner, step, over, aside(over)).wait_send()
+            far_copy(buffer, sent, got, step).wait_send()
             return carry
 
         lax.fori_loop(0, 8, body, 0)
@@ -249,8 +270,15 @@
         weighted = (gradient[...] - values[...]) * weight[...]
         pieces[iteration, sub] = three(basis[...], weighted, NT)
         gather_start(*block)
+
+        @pl.when(iteration == 0)
+        def _():
+            gather_forward(inverse, inverse_sent, inverse_got)
+
         product(weighted, dirichlet_high, dirichlet_low)
         gather_relay(*block)
+
+        gather_forward(*block)
 
         @pl.when(iteration == 0)
         def _():

time: 184 us -> 175 us (0.951)
  Pallas kernels: 170 us -> 161 us
    pallas_call x1, Pallas kernels: 170 us -> 161 us  [local(): pl.pallas_call(kernel, out_shape=jax.ShapeDtypeStruct((RHS, NI), F32), in...]
where the time goes in v3:
time: 175 us; the launch traced here: 174 us
  Pallas kernels  161 us (92%)
  local copies, waits for them, and re-layouts  6.92 us (4%)
  other arithmetic  6.44 us (4%)
    pallas_call x1, Pallas kernels, local(): pl.pallas_call(kernel, out_shape=jax.ShapeDtypeStruct((RHS, NI), F32), in...  161 us

profile of v3, /device:TPU:1, one launch (start us, length us, event | category | flops | bytes accessed | tf_op | source)
XLA Modules:
  0.0 174.4 jit_solution(18300021794634879340)
XLA Ops:
  0.0 0.5 broadcast.61
  0.5 1.3 reduce.3
  1.8 0.1 lt.48
  1.9 0.7 convert_bitcast_fusion
  2.6 1.3 divide_bitcast_fusion.weight
  3.9 0.1 lt.49
  4.0 0.7 squeeze.28
  4.7 0.6 compare_select_fusion.1.row_of
  5.3 0.1 broadcast_in_dim.16
  5.4 1.3 copy.14.my_owner
  6.7 1.5 pad_maximum_fusion.inverse_block
  8.2 0.6 lt.57
  8.9 1.3 squeeze.32
  10.2 1.0 compare_select_fusion.column_of
  11.2 161.1 %shard_map.100 = f32[192,1152]{1,0:T(8,128)} custom-call(f32[1152,1152]{1,0:T(8,128)} %bitcast.16, f32[1152,1152]{1,0:T(8,128)} %bitcast.17, f32[24,1152]{1,0:T(8,128)} %bitcast.21, f32[24,896]{1,0:T(8,128)} %pad_maximum_fusion.inverse_block, s32[24,1]{1,0:T(8,128)} %copy.14.my_owner, s32[2,1,768]{2,1,0:T(1,128)} %compare_select_fusion.1.row_of, ...), custom_call_target="tpu_custom_call" | custom-call | tf_op jit(solution)/shard_map/pallas_call | solution.py:320
  172.3 2.1 %copy.16 = f32[1,1,192,1152]{3,2,1,0:T(8,128)} copy(f32[1,1,192,1152]{3,2,1,0:T(8,128)} %bitcast.18) | data formatting | bytes 1769472
  (5 shorter events, 0.1 us)
